TPU v7x, 32 devices: a whole 2x2x4 slice. The times are simulated.
32 devices in a mesh: grp: 2 (over x), col: 16 (over z, y, core).
Axes of the slice: x: 2, y: 2, z: 4, core: 2. Of those that a mesh axis runs over, the one named last changes fastest.
Arguments:
- database: int32 [256, 4096], P('col', 'grp'), parts along dimension 1, may hold values from 0 to 255
- queries: int32 [16, 256], P('grp', 'col'), parts along dimension 0, may hold values from -2147483648 to 2147483646
- key_rows: int32 [16, 8192], P('grp', 'col'), parts along dimension 0, may hold values from -2147483648 to 2147483646
- hint: int32 [4, 1024], P('grp'), parts along dimension 0, may hold values from -2147483648 to 2147483646
- assignment: int32 [32], P('grp'), parts along dimension 0, may hold values from 0 to 15, each once
Outputs:
- packed: float32 [32, 2, 1024], P(('grp', 'col')), parts along dimension 0
There are 2 independent parts, one for each index of `grp`. A program takes and returns all parts, laid end to end along the dimension named above; each array names one. Nothing has to cross between parts.
Inputs may be any that keep to these rules, and one draw needn't show every extreme that they name: `assignment`: every unit appears in exactly one slot.
All inputs are finite; a program needn't handle non-finite values.
Results may differ from a plain program's by a relative error of at most 0.0003.
Values sent between devices are 32-bit elements; how exact they have to be, the bound alone decides.
A program may use at most 128 MiB of HBM per device.

v0:
```python
import jax
import jax.numpy as jnp
from jax import lax
from jax.sharding import PartitionSpec as P

LEVELS = 2
DIGITS = 2


def automorph(polynomial, galois):
    cycle_width = polynomial.shape[0]
    inverse = pow(galois, -1, 2 * cycle_width)
    source = jnp.arange(cycle_width, dtype=jnp.int32) * inverse % (2 * cycle_width)
    picked = jnp.take(polynomial, source % cycle_width, axis=0)
    return jnp.where(source < cycle_width, picked, -picked)


def toeplitz(key_poly):
    cycle_width = key_poly.shape[0]
    shifted = jnp.concatenate([-key_poly[1:], key_poly, -key_poly[:1]])
    tiled_rows = jnp.tile(shifted, cycle_width)[: cycle_width * (2 * cycle_width - 1)]
    return tiled_rows.reshape(cycle_width, 2 * cycle_width - 1)[
        :, cycle_width - 1 : 2 * cycle_width - 1
    ]


def switch_section(mask_poly, value_poly, section_keys, galois):
    cycle_width = mask_poly.shape[0]
    rotated_mask = automorph(mask_poly, galois)
    rotated_value = automorph(value_poly, galois)
    switched = jnp.zeros((2 * cycle_width,), jnp.int32)
    for digit_index in range(section_keys.shape[0]):
        digit_row = jnp.bitwise_and(jnp.right_shift(rotated_mask, 16 * digit_index), 65535)
        matrix = jnp.concatenate(
            [toeplitz(section_keys[digit_index, 0]), toeplitz(section_keys[digit_index, 1])], axis=1
        )
        switched = (
            switched + jnp.dot(digit_row[None, :], matrix, preferred_element_type=jnp.int32)[0]
        )
    return (mask_poly + switched[:cycle_width], value_poly + rotated_value + switched[cycle_width:])


def pack_unit(mask_poly, value_poly, key_row):
    cycle_width = mask_poly.shape[0]
    section_table = key_row.reshape(LEVELS, DIGITS, 2, cycle_width)
    for section_index in range(LEVELS):
        galois = cycle_width // 2**section_index + 1
        mask_poly, value_poly = switch_section(
            mask_poly, value_poly, section_table[section_index], galois
        )
    return jnp.stack([mask_poly, value_poly])


def split_words(words):
    lower_half = jnp.bitwise_and(words, 65535).astype(jnp.float32)
    upper_half = jnp.bitwise_and(jnp.right_shift(words, 16), 65535).astype(jnp.float32)
    return (lower_half, upper_half)


def join_words(lower_half, upper_half):
    return lower_half.astype(jnp.int32) + jnp.left_shift(upper_half.astype(jnp.int32), 16)


def on_device(database, queries, key_rows, hint, assignment):
    cycle_width = hint.shape[1]
    poly_count = hint.shape[0]
    slot_count = assignment.shape[0] // lax.axis_size("col")
    key_table = lax.all_gather(key_rows, "col", axis=1, tiled=True)
    partial_value = jnp.dot(queries, database, preferred_element_type=jnp.int32)
    owned_slots = lax.dynamic_slice_in_dim(
        assignment, lax.axis_index("col") * slot_count, slot_count
    )
    lower_half, upper_half = split_words(partial_value)
    lower_sum, upper_sum = lax.psum((lower_half, upper_half), "col")
    summed = join_words(lower_sum, upper_sum)
    value_rows = jnp.take(summed.reshape(-1, cycle_width), owned_slots, axis=0)

    def pack_one(inputs):
        unit_index, value_poly = inputs
        client = unit_index // poly_count
        poly_index = unit_index % poly_count
        mask_poly = lax.dynamic_index_in_dim(hint, poly_index, 0, keepdims=False)
        key_row = lax.dynamic_index_in_dim(key_table, client, 0, keepdims=False)
        return pack_unit(mask_poly, value_poly, key_row)

    packed_words = lax.map(pack_one, (owned_slots, value_rows))
    return packed_words.astype(jnp.float32) * 2.0 ** (-32)


def solution(mesh):
    placed = (P("col", "grp"), P("grp", "col"), P("grp", "col"), P("grp", None), P("grp"))
    return jax.shard_map(
        on_device,
        mesh=mesh,
        in_specs=placed,
        out_specs=P(("grp", "col"), None, None),
        check_vma=False,
    )
```

profile of v0, /device:TPU:0, one launch (start us, length us, event | category | flops | bytes accessed | tf_op | source)
XLA Modules:
  0.0 325.9 jit_solution(6749545963673076256)
XLA Ops:
  6.5 0.9 copy-done
  7.4 1.6 and_convert_fusion.1
  9.1 1.2 dynamic_slice.19
  12.9 24.2 %all_gather.3 = s32[8,8192]{1,0:T(8,128)S(1)} all-gather(s32[8,512]{1,0:T(8,128)} %param.9), channel_id=1, replica_groups=mesh['grp'=2,'col'=16] {'col'}, dimensions={1}, use_global_device_ids=true | all-gather | bytes 278528 | tf_op jit(solution)/shard_map/all_gather | solution.py:68
  37.1 0.1 dynamic-slice_reduce_fusion
  37.2 0.1 slice_negate_fusion.5
  37.3 0.6 fusion.37
  38.0 0.1 slice_negate_fusion.1
  38.1 0.6 fusion.35
  39.3 0.1 concatenate.58
  39.4 1.0 broadcast_bitcast_fusion.5
  40.4 2.0 copy.8
  42.4 3.7 %slice.292 = s32[2096128]{0:T(1024)} slice(s32[2097152]{0:T(1024)S(1)} %bitcast.75), slice={[0:2096128]} | slice | bytes 16769024 | tf_op jit(solution)/shard_map/while/body/eval_jaxpr/slice | solution.py:21
  46.2 12.3 %reshape.150 = s32[1024,2047]{1,0:T(8,128)} reshape(s32[2096128]{0:T(1024)} %slice.292) | data formatting | bytes 16769024 | tf_op jit(solution)/shard_map/while/body/eval_jaxpr/reshape | solution.py:22
  58.5 5.5 %slice.293 = s32[1024,1024]{1,0:T(8,128)} slice(s32[1024,2047]{1,0:T(8,128)} %reshape.150), slice={[0:1024], [1023:2047]} | slice | bytes 8388608 | tf_op jit(solution)/shard_map/while/body/eval_jaxpr/slice | solution.py:22
  64.7 0.1 concatenate.59
  64.8 1.0 broadcast_bitcast_fusion.4
  65.9 2.0 copy.9
  67.9 3.7 %slice.297 = s32[2096128]{0:T(1024)} slice(s32[2097152]{0:T(1024)S(1)} %bitcast.76), slice={[0:2096128]} | slice | bytes 16769024 | tf_op jit(solution)/shard_map/while/body/eval_jaxpr/slice | solution.py:21
  71.6 12.3 %reshape.151 = s32[1024,2047]{1,0:T(8,128)} reshape(s32[2096128]{0:T(1024)} %slice.297) | data formatting | bytes 16769024 | tf_op jit(solution)/shard_map/while/body/eval_jaxpr/reshape | solution.py:22
  83.9 5.5 %slice.298 = s32[1024,1024]{1,0:T(8,128)} slice(s32[1024,2047]{1,0:T(8,128)} %reshape.151), slice={[0:1024], [1023:2047]} | slice | bytes 8388608 | tf_op jit(solution)/shard_map/while/body/eval_jaxpr/slice | solution.py:22
  89.4 4.5 %gather_fusion = s32[1024]{0:T(1024)S(1)} fusion(s32[1024]{0:T(1024)S(1)} %bitcast.69, s32[1024]{0:T(1024)S(1)} %broadcast_clamp_fusion.1), kind=kCustom, calls=%fused_computation.clone | custom fusion | bytes 12288 | tf_op jit(solution)/shard_map/while/body/eval_jaxpr/jit(_take)/gather | solution.py:14
  94.6 1.0 broadcast_bitcast_fusion.7
  95.7 2.0 copy.6
  97.7 4.0 %slice.282 = s32[2096128]{0:T(1024)} slice(s32[2097152]{0:T(1024)S(1)} %bitcast.77), slice={[0:2096128]} | slice | bytes 16769024 | tf_op jit(solution)/shard_map/while/body/eval_jaxpr/slice | solution.py:21
  101.7 12.3 %reshape.148 = s32[1024,2047]{1,0:T(8,128)} reshape(s32[2096128]{0:T(1024)} %slice.282) | data formatting | bytes 16769024 | tf_op jit(solution)/shard_map/while/body/eval_jaxpr/reshape | solution.py:22
  114.0 5.4 %slice.283 = s32[1024,1024]{1,0:T(8,128)} slice(s32[1024,2047]{1,0:T(8,128)} %reshape.148), slice={[0:1024], [1023:2047]} | slice | bytes 8388608 | tf_op jit(solution)/shard_map/while/body/eval_jaxpr/slice | solution.py:22
  120.0 0.1 concatenate.56
  120.1 1.0 broadcast_bitcast_fusion.6
  121.2 2.0 copy.7
  123.2 3.7 %slice.287 = s32[2096128]{0:T(1024)} slice(s32[2097152]{0:T(1024)S(1)} %bitcast.78), slice={[0:2096128]} | slice | bytes 16769024 | tf_op jit(solution)/shard_map/while/body/eval_jaxpr/slice | solution.py:21
  126.9 12.3 %reshape.149 = s32[1024,2047]{1,0:T(8,128)} reshape(s32[2096128]{0:T(1024)} %slice.287) | data formatting | bytes 16769024 | tf_op jit(solution)/shard_map/while/body/eval_jaxpr/reshape | solution.py:22
  139.2 5.4 %slice.288 = s32[1024,1024]{1,0:T(8,128)} slice(s32[1024,2047]{1,0:T(8,128)} %reshape.149), slice={[0:1024], [1023:2047]} | slice | bytes 8388608 | tf_op jit(solution)/shard_map/while/body/eval_jaxpr/slice | solution.py:22
  145.2 0.1 concatenate.64
  145.3 4.3 %broadcast_bitcast_fusion.1 = s32[128,16,8,128]{3,2,1,0:T(8,128)} fusion(s32[2048]{0:T(1024)S(1)} %concatenate.64), kind=kLoop, calls=%fused_computation.21 | loop fusion | bytes 8396800
  150.3 4.3 %broadcast_bitcast_fusion = s32[128,16,8,128]{3,2,1,0:T(8,128)} fusion(s32[2048]{0:T(1024)S(1)} %concatenate.65), kind=kLoop, calls=%fused_computation.20 | loop fusion | bytes 8396800
  155.3 4.3 %broadcast_bitcast_fusion.3 = s32[128,16,8,128]{3,2,1,0:T(8,128)} fusion(s32[2048]{0:T(1024)S(1)} %concatenate.61), kind=kLoop, calls=%fused_computation.23 | loop fusion | bytes 8396800
  160.3 5.3 %broadcast_bitcast_fusion.2 = s32[128,16,8,128]{3,2,1,0:T(8,128)} fusion(s32[2048]{0:T(1024)S(1)} %concatenate.62), kind=kLoop, calls=%fused_computation.22 | loop fusion | bytes 8396800
  165.6 1.2 copy-done.3
  166.8 7.0 %fusion.4 = s32[1,2048]{1,0:T(1,128)S(1)} fusion(s32[1024,1]{0,1:T(1,128)S(1)} %bitcast.88, s32[1024,1024]{1,0:T(8,128)S(1)} %copy-done.3, s32[1024,1024]{1,0:T(8,128)S(1)} %copy-done.2), kind=kOutput, calls=%fused_computation.8 | convolution fusion | flops 6291456 | bytes 8400896 | tf_op jit(solution)/shard_map/while/body/eval_jaxpr/dot_general | solution.py:38
  173.8 6.8 %fusion = s32[1,2048]{1,0:T(1,128)S(1)} fusion(s32[1024,1]{0,1:T(1,128)S(1)} %bitcast.87, s32[1024,1024]{1,0:T(8,128)S(1)} %copy-done.7, s32[1024,1024]{1,0:T(8,128)S(1)} %copy-done.4), kind=kOutput, calls=%fused_computation.4 | convolution fusion | flops 6291456 | bytes 8400896 | tf_op jit(solution)/shard_map/while/body/eval_jaxpr/dot_general | solution.py:38
  182.6 2.4 copy.12
  185.0 3.5 %slice.313 = s32[2096128]{0:T(1024)} slice(s32[2097152]{0:T(1024)S(1)} %bitcast.79), slice={[0:2096128]} | slice | bytes 16769024 | tf_op jit(solution)/shard_map/while/body/eval_jaxpr/slice | solution.py:21
  188.5 12.3 %reshape.154 = s32[1024,2047]{1,0:T(8,128)} reshape(s32[2096128]{0:T(1024)} %slice.313) | data formatting | bytes 16769024 | tf_op jit(solution)/shard_map/while/body/eval_jaxpr/reshape | solution.py:22
  200.8 5.5 %slice.314 = s32[1024,1024]{1,0:T(8,128)} slice(s32[1024,2047]{1,0:T(8,128)} %reshape.154), slice={[0:1024], [1023:2047]} | slice | bytes 8388608 | tf_op jit(solution)/shard_map/while/body/eval_jaxpr/slice | solution.py:22
  206.4 5.4 %copy.13 = s32[128,16,8,128]{3,1,2,0:T(8,128)S(1)} copy(s32[128,16,8,128]{3,2,1,0:T(8,128)} %broadcast_bitcast_fusion) | data formatting | bytes 16777216
  211.8 3.7 %slice.318 = s32[2096128]{0:T(1024)} slice(s32[2097152]{0:T(1024)S(1)} %bitcast.80), slice={[0:2096128]} | slice | bytes 16769024 | tf_op jit(solution)/shard_map/while/body/eval_jaxpr/slice | solution.py:21
  215.4 12.3 %reshape.155 = s32[1024,2047]{1,0:T(8,128)} reshape(s32[2096128]{0:T(1024)} %slice.318) | data formatting | bytes 16769024 | tf_op jit(solution)/shard_map/while/body/eval_jaxpr/reshape | solution.py:22
  227.8 5.5 %slice.319 = s32[1024,1024]{1,0:T(8,128)} slice(s32[1024,2047]{1,0:T(8,128)} %reshape.155), slice={[0:1024], [1023:2047]} | slice | bytes 8388608 | tf_op jit(solution)/shard_map/while/body/eval_jaxpr/slice | solution.py:22
  233.2 5.4 %copy.10 = s32[128,16,8,128]{3,1,2,0:T(8,128)S(1)} copy(s32[128,16,8,128]{3,2,1,0:T(8,128)} %broadcast_bitcast_fusion.3) | data formatting | bytes 16777216
  238.6 3.7 %slice.303 = s32[2096128]{0:T(1024)} slice(s32[2097152]{0:T(1024)S(1)} %bitcast.81), slice={[0:2096128]} | slice | bytes 16769024 | tf_op jit(solution)/shard_map/while/body/eval_jaxpr/slice | solution.py:21
  242.3 12.3 %reshape.152 = s32[1024,2047]{1,0:T(8,128)} reshape(s32[2096128]{0:T(1024)} %slice.303) | data formatting | bytes 16769024 | tf_op jit(solution)/shard_map/while/body/eval_jaxpr/reshape | solution.py:22
  254.6 5.4 %slice.304 = s32[1024,1024]{1,0:T(8,128)} slice(s32[1024,2047]{1,0:T(8,128)} %reshape.152), slice={[0:1024], [1023:2047]} | slice | bytes 8388608 | tf_op jit(solution)/shard_map/while/body/eval_jaxpr/slice | solution.py:22
  260.0 5.4 %copy.11 = s32[128,16,8,128]{3,1,2,0:T(8,128)S(1)} copy(s32[128,16,8,128]{3,2,1,0:T(8,128)} %broadcast_bitcast_fusion.2) | data formatting | bytes 16777216
  265.4 3.7 %slice.308 = s32[2096128]{0:T(1024)} slice(s32[2097152]{0:T(1024)S(1)} %bitcast.82), slice={[0:2096128]} | slice | bytes 16769024 | tf_op jit(solution)/shard_map/while/body/eval_jaxpr/slice | solution.py:21
  269.2 12.3 %reshape.153 = s32[1024,2047]{1,0:T(8,128)} reshape(s32[2096128]{0:T(1024)} %slice.308) | data formatting | bytes 16769024 | tf_op jit(solution)/shard_map/while/body/eval_jaxpr/reshape | solution.py:22
  281.5 5.4 %slice.309 = s32[1024,1024]{1,0:T(8,128)} slice(s32[1024,2047]{1,0:T(8,128)} %reshape.153), slice={[0:1024], [1023:2047]} | slice | bytes 8388608 | tf_op jit(solution)/shard_map/while/body/eval_jaxpr/slice | solution.py:22
  287.0 0.9 shift-left_add_fusion
  287.9 4.5 %gather_fusion.2 = s32[1024]{0:T(1024)S(1)} fusion(s32[1024]{0:T(1024)S(1)} %bitcast.71, s32[1024]{0:T(1024)S(1)} %broadcast_clamp_fusion.1), kind=kCustom, calls=%fused_computation.2.clone | custom fusion | bytes 12288 | tf_op jit(solution)/shard_map/while/body/eval_jaxpr/jit(_take)/gather | solution.py:14
  292.5 4.5 %gather_fusion.3 = s32[1024]{0:T(1024)S(1)} fusion(s32[1024]{0:T(1024)S(1)} %get-tuple-element.68, s32[1024]{0:T(1024)S(1)} %get-tuple-element.73), kind=kCustom, calls=%fused_computation.3.clone | custom fusion | bytes 12288 | tf_op jit(solution)/shard_map/while/body/eval_jaxpr/jit(_take)/gather | solution.py:14
  297.0 4.5 %gather_fusion.1 = s32[1024]{0:T(1024)S(1)} fusion(s32[1024]{0:T(1024)S(1)} %get-tuple-element.67, s32[1024]{0:T(1024)S(1)} %get-tuple-element.73), kind=kCustom, calls=%fused_computation.1.clone | custom fusion | bytes 12288 | tf_op jit(solution)/shard_map/while/body/eval_jaxpr/jit(_take)/gather | solution.py:14
  301.6 9.5 %fusion.12 = s32[1,2048]{1,0:T(1,128)S(1)} fusion(s32[1024,1]{0,1:T(1,128)S(1)} %bitcast.90, s32[1024,1024]{1,0:T(8,128)} %slice.319, s32[1024,1024]{1,0:T(8,128)} %slice.314), kind=kOutput, calls=%fused_computation.16 | convolution fusion | flops 6291456 | bytes 8400896 | tf_op jit(solution)/shard_map/while/body/eval_jaxpr/dot_general | solution.py:38
  311.1 6.8 %fusion.8 = s32[1,2048]{1,0:T(1,128)S(1)} fusion(s32[1024,1]{0,1:T(1,128)S(1)} %bitcast.89, s32[1024,1024]{1,0:T(8,128)S(1)} %copy-done.6, s32[1024,1024]{1,0:T(8,128)S(1)} %copy-done.5), kind=kOutput, calls=%fused_computation.12 | convolution fusion | flops 6291456 | bytes 8400896 | tf_op jit(solution)/shard_map/while/body/eval_jaxpr/dot_general | solution.py:38
  317.9 0.6 fusion.16
  (42 shorter events, 0.6 us)
Async XLA Ops:
  6.5 0.9 copy-start
  6.5 280.4 %all-reduce.3.cloned.1.call-start = ((), (), s32[]{:S(2)}) async-start(), calls=%async_computation | async-start | bytes 262144 | tf_op jit(solution)/shard_map/psum | solution.py:74
  83.9 5.5 %copy-start.8 = (s32[2,1024]{1,0:T(2,128)S(1)}, s32[2,1024]{1,0:T(2,128)}, u32[]{:S(2)}) copy-start(s32[2,1024]{1,0:T(2,128)} %param.10) | copy-start | bytes 24580
  160.3 5.3 %copy-start.2 = (s32[1024,1024]{1,0:T(8,128)S(1)}, s32[1024,1024]{1,0:T(8,128)}, u32[]{:S(2)}) copy-start(s32[1024,1024]{1,0:T(8,128)} %slice.293) | copy-start | bytes 12582916
  160.3 6.5 %copy-start.3 = (s32[1024,1024]{1,0:T(8,128)S(1)}, s32[1024,1024]{1,0:T(8,128)}, u32[]{:S(2)}) copy-start(s32[1024,1024]{1,0:T(8,128)} %slice.298) | copy-start | bytes 12582916
  160.3 13.5 %copy-start.4 = (s32[1024,1024]{1,0:T(8,128)S(1)}, s32[1024,1024]{1,0:T(8,128)}, u32[]{:S(2)}) copy-start(s32[1024,1024]{1,0:T(8,128)} %slice.283) | copy-start | bytes 12582916
  160.3 13.5 %copy-start.7 = (s32[1024,1024]{1,0:T(8,128)S(1)}, s32[1024,1024]{1,0:T(8,128)}, u32[]{:S(2)}) copy-start(s32[1024,1024]{1,0:T(8,128)} %slice.288) | copy-start | bytes 12582916
  166.8 15.7 %slice-start = ((s8[8388608]{0:T(1024)(128)(4,1)}), s8[4194304]{0:T(1024)(128)(4,1)S(1)}, s32[]{:S(2)}) async-start(s8[8388608]{0:T(1024)(128)(4,1)} %bitcast.73), calls=%async_computation.1 | async-start | bytes 8388608
  173.8 8.7 %slice-start.1 = ((s8[8388608]{0:T(1024)(128)(4,1)}), s8[4194304]{0:T(1024)(128)(4,1)S(1)}, s32[]{:S(2)}) async-start(s8[8388608]{0:T(1024)(128)(4,1)} %bitcast.73), calls=%async_computation.2 | async-start | bytes 8388608
  301.5 9.6 %copy-start.5 = (s32[1024,1024]{1,0:T(8,128)S(1)}, s32[1024,1024]{1,0:T(8,128)}, u32[]{:S(2)}) copy-start(s32[1024,1024]{1,0:T(8,128)} %slice.304) | copy-start | bytes 12582916
  301.6 9.6 %copy-start.6 = (s32[1024,1024]{1,0:T(8,128)S(1)}, s32[1024,1024]{1,0:T(8,128)}, u32[]{:S(2)}) copy-start(s32[1024,1024]{1,0:T(8,128)} %slice.309) | copy-start | bytes 12582916
  301.6 17.0 %copy-start.1 = (s32[16,2048]{1,0:T(8,128)S(1)}, s32[16,2048]{1,0:T(8,128)}, u32[]{:S(2)}) copy-start(s32[16,2048]{1,0:T(8,128)} %param.7) | copy-start | bytes 393220
Sparse Core Ops, SparseCore 0:
  10.9 91.1 all-reduce.2
where the time goes:
time: 330 us; the launch traced here: 326 us
  local copies, waits for them, and re-layouts  244 us (74%)
  matrix products  31.6 us (10%)
  blocking collectives  24.2 us (7%)
  between operations  23.8 us (7%)
    reshape x8, local copies, waits for them, and re-layouts, toeplitz(): tiled_rows.reshape(cycle_width, 2 * cycle_width - 1)  98.5 us
    unnamed x38, local copies, waits for them, and re-layouts  51 us
    slice x8, local copies, waits for them, and re-layouts, toeplitz(): tiled_rows.reshape(cycle_width, 2 * cycle_width - 1)  43.7 us
    dot_general x4, matrix products, switch_section(): jnp.dot(digit_row[None, :], matrix, preferred_element_type=jnp.int32)[0]  30 us
    slice x8, local copies, waits for them, and re-layouts, toeplitz(): jnp.tile(shifted, cycle_width)[:cycle_width * (2 * cycle_width - 1)]  29.8 us
    all_gather x1, blocking collectives, on_device(): key_table = lax.all_gather(key_rows, 'col', axis=1, tiled=True)  24.2 us
    gather x4, local copies, waits for them, and re-layouts, automorph(): picked = jnp.take(polynomial, source % cycle_width, axis=0)  18.1 us
  transfers between devices with their start and end apart: 1, of which 0 were waited for; matrix products, arithmetic and copies ran while one was open for 74% of the time, Pallas kernels for 0%

commit v1 on v0

v1 whole, which is shorter than its diff:
```python
import functools

import jax
import jax.numpy as jnp
from jax import lax
from jax.experimental import pallas as pl
from jax.experimental.pallas import tpu as pltpu
from jax.sharding import PartitionSpec as P

LEVELS = 2
DIGITS = 2
LANES = 128
WORD_BYTES = 4
DIGIT_BYTES = WORD_BYTES // DIGITS


def iota(shape, axis):
    return lax.broadcasted_iota(jnp.int32, shape, axis)


def byte_of(words, index):
    return jnp.bitwise_and(jnp.right_shift(words, 8 * index), 255).astype(jnp.float32)


def shifted(poly, amount):
    rows = poly.shape[0]
    amount = amount % (2 * rows * LANES)
    negate, turn = divmod(amount // LANES, rows)
    moved = poly
    if turn:
        moved = pltpu.roll(poly, turn, 0)
        moved = jnp.where(iota(poly.shape, 0) >= turn, moved, -moved)
    return -moved if negate else moved


def automorph(poly, level):
    step = poly.shape[0] * LANES >> level
    period = 2 << level
    residue = jnp.bitwise_and(iota(poly.shape, 1), period - 1)
    out = poly
    for m in range(1, period):
        out = jnp.where(residue == m, shifted(poly, step * m), out)
    return out


def fill_toeplitz(word_poly, toeplitz):
    rows = word_poly.shape[0]
    square = (LANES, LANES)
    ahead = iota(square, 1) >= iota(square, 0)

    def turned(q):
        row = jnp.broadcast_to(word_poly[q : q + 1], square)
        return pltpu.roll(row, 0, 1, stride=1, stride_axis=0)

    before = turned(rows - 1)
    for q in range(rows):
        here = turned(q)
        words = jnp.where(ahead, here, before)
        for t in range(DIGITS):
            for a in range(DIGIT_BYTES):
                part = byte_of(words, t * DIGIT_BYTES + a)
                if q == 0:
                    part = jnp.where(ahead, part, -part)
                toeplitz[t, a * LANES : (a + 1) * LANES, q * LANES : (q + 1) * LANES] = part.astype(
                    jnp.bfloat16
                )
        before = here


def key_side(keys):
    zero = jnp.zeros(keys[0].shape, jnp.float32)
    columns = []
    for a in range(DIGIT_BYTES):
        blocks = [byte_of(k, s - a) if s >= a else zero for s in range(WORD_BYTES) for k in keys]
        columns.append(jnp.concatenate(blocks, axis=0))
    return jnp.concatenate(columns, axis=1).astype(jnp.bfloat16)


def switch(toeplitz, key_polys, rows):
    cycle = rows * LANES
    products = [
        jnp.dot(key_side(key_polys[t]), toeplitz[t], preferred_element_type=jnp.float32).astype(jnp.int32)
        for t in range(DIGITS)
    ]
    sums = []
    for p in range(2):
        words = jnp.zeros((rows, cycle), jnp.int32)
        for s in range(WORD_BYTES):
            at = (s * 2 + p) * rows
            total = products[0][at : at + rows]
            for t in range(1, DIGITS):
                total = total + products[t][at : at + rows]
            words = words + jnp.left_shift(total, 8 * s)
        out = jnp.zeros((rows, LANES), jnp.int32)
        for q in range(rows):
            out = out + shifted(words[:, q * LANES : (q + 1) * LANES], q * LANES)
        sums.append(out)
    return sums


def kernel(
    n, slots, share, assign, database, queries, keys, hint, out,
    part, unit_part, unit_keys, unit_masks, ans_send, key_send, ans_recv, key_recv, key_words, toeplitz,
    ans_sent, key_sent, ans_got, key_got,
):
    me = lax.axis_index("col")
    clients, columns = queries.shape
    polys, cycle = hint.shape
    rows = cycle // LANES
    key_rows = unit_keys.shape[1]
    barrier = pltpu.get_barrier_semaphore()

    def greet(i, carry):
        pl.semaphore_signal(barrier, inc=1, device_id={"col": lax.rem(me + i, n)})
        return carry

    lax.fori_loop(1, n, greet, 0)

    lane_owner = iota((clients, LANES), 1) // (LANES // share)
    for j in range(key_rows):
        tile = keys[:, j * LANES : (j + 1) * LANES]
        if share > 1:
            tile = jnp.where(lane_owner == lax.rem(me, share), tile, 0)
        for c in range(clients):
            for p in range(polys):
                unit_keys[c * polys + p, j : j + 1, :] = tile[c : c + 1]

    for p in range(polys):
        for q in range(rows):
            row = hint[p : p + 1, q * LANES : (q + 1) * LANES]
            for c in range(clients):
                unit_masks[c * polys + p, q : q + 1, :] = row

    query_words = queries[...]
    query_bytes = jnp.concatenate([byte_of(query_words, b) for b in range(WORD_BYTES)], axis=0)
    products = jnp.dot(
        query_bytes.astype(jnp.bfloat16),
        database[...].astype(jnp.float32).astype(jnp.bfloat16),
        preferred_element_type=jnp.float32,
    ).astype(jnp.int32)
    partial = products[:clients]
    for b in range(1, WORD_BYTES):
        partial = partial + jnp.left_shift(products[b * clients : (b + 1) * clients], 8 * b)
    for j in range(polys * rows):
        part[j * clients : (j + 1) * clients, :] = partial[:, j * LANES : (j + 1) * LANES]

    for c in range(clients):
        for p in range(polys):
            unit_part[c * polys + p] = part[pl.ds(p * rows * clients + c, rows, stride=clients), :]

    def stage_into(ans, key, at, owner):
        for k in range(slots):
            unit = assign[owner * slots + k]
            ans[at, k * rows : (k + 1) * rows, :] = unit_part[unit]
            key[at, k * key_rows : (k + 1) * key_rows, :] = unit_keys[unit]

    def stage(i, carry):
        owner = lax.rem(me + i, n)
        stage_into(ans_send, key_send, owner, owner)
        return carry

    lax.fori_loop(1, n, stage, 0)
    stage_into(ans_recv, key_recv, me, me)

    pl.semaphore_wait(barrier, n - 1)

    def key_copy(there, slot):
        return pltpu.make_async_remote_copy(
            src_ref=key_send.at[there],
            dst_ref=key_recv.at[slot],
            send_sem=key_sent.at[there],
            recv_sem=key_got.at[slot],
            device_id={"col": there},
        )

    def ans_copy(there, slot):
        return pltpu.make_async_remote_copy(
            src_ref=ans_send.at[there],
            dst_ref=ans_recv.at[slot],
            send_sem=ans_sent.at[there],
            recv_sem=ans_got.at[slot],
            device_id={"col": there},
        )

    def send_keys(i, carry):
        key_copy(lax.rem(me + i, n), me).start()
        return carry

    def send_answers(i, carry):
        ans_copy(lax.rem(me + i, n), me).start()
        return carry

    def got_keys(i, carry):
        there = lax.rem(me + i, n)
        key_copy(there, there).wait_recv()
        return carry

    def got_answers(i, carry):
        there = lax.rem(me + i, n)
        ans_copy(there, there).wait_recv()
        return carry

    def sent(i, carry):
        there = lax.rem(me + i, n)
        key_copy(there, me).wait_send()
        ans_copy(there, me).wait_send()
        return carry

    lax.fori_loop(1, n, send_keys, 0)
    lax.fori_loop(1, n, send_answers, 0)

    switched = []
    for k in range(slots):
        mask = unit_masks[assign[me * slots + k]]
        fill_toeplitz(automorph(mask, 0), toeplitz)
        if k == 0:
            lax.fori_loop(1, n, got_keys, 0)
        for j in range(n // share):
            block = key_recv[j * share, k * key_rows : (k + 1) * key_rows, :]
            for h in range(1, share):
                block = block + key_recv[j * share + h, k * key_rows : (k + 1) * key_rows, :]
            key_words[j * key_rows : (j + 1) * key_rows, :] = block
        added = []
        for level in range(LEVELS):
            if level:
                fill_toeplitz(automorph(mask, level), toeplitz)

            def key_poly(t, p):
                at = ((level * DIGITS + t) * 2 + p) * rows
                return key_words[at : at + rows, :]

            to_mask, to_value = switch(
                toeplitz, [[key_poly(t, p) for p in range(2)] for t in range(DIGITS)], rows
            )
            mask = mask + to_mask
            added.append(to_value)
        switched.append((mask, added))

    lax.fori_loop(1, n, got_answers, 0)
    for k, (mask, added) in enumerate(switched):
        value = ans_recv[0, k * rows : (k + 1) * rows, :]
        for j in range(1, n):
            value = value + ans_recv[j, k * rows : (k + 1) * rows, :]
        for level in range(LEVELS):
            value = value + automorph(value, level) + added[level]
        for index, words in enumerate((mask, value)):
            scaled = words.astype(jnp.float32) * 2.0 ** (-32)
            for q in range(rows):
                out[k, index : index + 1, q * LANES : (q + 1) * LANES] = scaled[q : q + 1]
    lax.fori_loop(1, n, sent, 0)


def solution(mesh):
    n = mesh.shape["col"]

    def on_device(database, queries, key_rows, hint, assignment):
        clients = queries.shape[0]
        polys, cycle = hint.shape
        rows = cycle // LANES
        slots = assignment.shape[0] // n
        width = key_rows.shape[1]
        share = max(1, LANES // width)
        if share > 1:
            key_rows = jnp.tile(key_rows, (1, share))
        tiles = key_rows.shape[1] // LANES
        vmem = pl.BlockSpec(memory_space=pltpu.VMEM)
        return pl.pallas_call(
            functools.partial(kernel, n, slots, share),
            out_shape=jax.ShapeDtypeStruct((slots, 2, cycle), jnp.float32),
            in_specs=[pl.BlockSpec(memory_space=pltpu.SMEM), vmem, vmem, vmem, vmem],
            out_specs=vmem,
            scratch_shapes=[
                pltpu.VMEM((polys * rows * clients, LANES), jnp.int32),
                pltpu.VMEM((polys * clients, rows, LANES), jnp.int32),
                pltpu.VMEM((polys * clients, tiles, LANES), jnp.int32),
                pltpu.VMEM((polys * clients, rows, LANES), jnp.int32),
                pltpu.VMEM((n, slots * rows, LANES), jnp.int32),
                pltpu.VMEM((n, slots * tiles, LANES), jnp.int32),
                pltpu.VMEM((n, slots * rows, LANES), jnp.int32),
                pltpu.VMEM((n, slots * tiles, LANES), jnp.int32),
                pltpu.VMEM((n // share * tiles, LANES), jnp.int32),
                pltpu.VMEM((DIGITS, DIGIT_BYTES * LANES, cycle), jnp.bfloat16),
                pltpu.SemaphoreType.DMA((n,)),
                pltpu.SemaphoreType.DMA((n,)),
                pltpu.SemaphoreType.DMA((n,)),
                pltpu.SemaphoreType.DMA((n,)),
            ],
            compiler_params=pltpu.CompilerParams(collective_id=0, has_side_effects=True),
        )(assignment, database, queries, key_rows, hint)

    placed = (P("col", "grp"), P("grp", "col"), P("grp", "col"), P("grp", None), P("grp"))
    return jax.shard_map(
        on_device,
        mesh=mesh,
        in_specs=placed,
        out_specs=P(("grp", "col"), None, None),
        check_vma=False,
    )
```

time: 330 us -> 13.5 us (0.04); the launches traced: 326 us -> 13.3 us
  local copies, waits for them, and re-layouts: 244 us -> 1.3 us
  matrix products: 31.6 us -> 0 us
  blocking collectives: 24.2 us -> 0 us
  between operations: 23.8 us -> 0.01 us
  Pallas kernels: 0 us -> 12 us
    reshape x9 -> x0, local copies, waits for them, and re-layouts: 98.5 us -> none  [the longest x8 98.5 us: toeplitz(): tiled_rows.reshape(cycle_width, 2 * cycle_width - 1)]
    slice x21 -> x0, local copies, waits for them, and re-layouts: 74.9 us -> none  [the longest x8 43.7 us: toeplitz(): tiled_rows.reshape(cycle_width, 2 * cycle_width - 1)]
    unnamed x38 -> x1, local copies, waits for them, and re-layouts: 51 us -> 1.3 us
    dot_general x5 -> x0, matrix products: 31.6 us -> none  [the longest x4 30 us: switch_section(): jnp.dot(digit_row[None, :], matrix, preferred_element_type=jnp.int32)[0]]
    all_gather x1 -> x0, blocking collectives: 24.2 us -> none  [on_device(): key_table = lax.all_gather(key_rows, 'col', axis=1, tiled=True)]
    gather x4 -> x0, local copies, waits for them, and re-layouts: 18.1 us -> none  [automorph(): picked = jnp.take(polynomial, source % cycle_width, axis=0)]
    pallas_call x0 -> x1, Pallas kernels: none -> 12 us  [on_device(): pl.pallas_call(functools.partial(kernel, n, slots, share), out_shape=jax....]
  transfers between devices with their start and end apart: 1 -> 0, of which waited for: 0 -> 0; matrix products, arithmetic and copies ran while one was open for 74% -> 0% of each run, Pallas kernels for 0% -> 0%
where the time goes in v1:
time: 13.5 us; the launch traced here: 13.3 us
  Pallas kernels  12 us (89%)
  local copies, waits for them, and re-layouts  1.3 us (10%)
    pallas_call x1, Pallas kernels, on_device(): pl.pallas_call(functools.partial(kernel, n, slots, share), out_shape=jax....  12 us
    unnamed x1, local copies, waits for them, and re-layouts  1.3 us

profile of v1, /device:TPU:0, one launch (start us, length us, event | category | flops | bytes accessed | tf_op | source)
XLA Modules:
  0.0 13.3 jit_solution(5578578397920472018)
XLA Ops:
  0.0 12.0 %shard_map.55 = f32[1,2,1024]{2,1,0:T(2,128)} custom-call(s32[16]{0:T(128)} %assign.1, s32[16,2048]{1,0:T(8,128)} %database.1, s32[8,16]{1,0:T(8,128)} %queries.1, s32[8,512]{1,0:T(8,128)} %keys.1, s32[2,1024]{1,0:T(2,128)} %hint.1), custom_call_target="tpu_custom_call" | custom-call | tf_op jit(solution)/shard_map/pallas_call | solution.py:267
  12.0 1.3 %copy.7 = f32[1,2,1024]{2,1,0:T(2,128)} copy(f32[1,2,1024]{2,1,0:T(2,128)} %shard_map.55) | data formatting | bytes 16384

commit v2 on v1

--- a/solution.py
+++ b/solution.py
@@ -99,8 +99,8 @@
 
 
 def kernel(
-    n, slots, share, assign, database, queries, keys, hint, out,
-    part, unit_part, unit_keys, unit_masks, ans_send, key_send, ans_recv, key_recv, key_words, toeplitz,
+    n, slots, share, assign_hbm, database_hbm, queries_hbm, keys_hbm, hint_hbm, out,
+    assign, database, queries, keys, hint, loaded, part, unit_part, unit_keys, unit_masks, ans_send, key_send, ans_recv, key_recv, key_words, toeplitz,
     ans_sent, key_sent, ans_got, key_got,
 ):
     me = lax.axis_index("col")
@@ -116,6 +116,22 @@
 
     lax.fori_loop(1, n, greet, 0)
 
+    loads = [
+        pltpu.make_async_copy(source, target, loaded.at[i])
+        for i, (source, target) in enumerate(
+            (
+                (keys_hbm, keys),
+                (hint_hbm, hint),
+                (assign_hbm, assign),
+                (queries_hbm, queries),
+                (database_hbm, database),
+            )
+        )
+    ]
+    for load in loads:
+        load.start()
+
+    loads[0].wait()
     lane_owner = iota((clients, LANES), 1) // (LANES // share)
     for j in range(key_rows):
         tile = keys[:, j * LANES : (j + 1) * LANES]
@@ -125,12 +141,15 @@
             for p in range(polys):
                 unit_keys[c * polys + p, j : j + 1, :] = tile[c : c + 1]
 
+    loads[1].wait()
     for p in range(polys):
         for q in range(rows):
             row = hint[p : p + 1, q * LANES : (q + 1) * LANES]
             for c in range(clients):
                 unit_masks[c * polys + p, q : q + 1, :] = row
 
+    for load in loads[2:]:
+        load.wait()
     query_words = queries[...]
     query_bytes = jnp.concatenate([byte_of(query_words, b) for b in range(WORD_BYTES)], axis=0)
     products = jnp.dot(
@@ -263,13 +282,19 @@
         if share > 1:
             key_rows = jnp.tile(key_rows, (1, share))
         tiles = key_rows.shape[1] // LANES
-        vmem = pl.BlockSpec(memory_space=pltpu.VMEM)
+        place = pl.BlockSpec(memory_space=pltpu.HBM)
         return pl.pallas_call(
             functools.partial(kernel, n, slots, share),
-            out_shape=jax.ShapeDtypeStruct((slots, 2, cycle), jnp.float32),
-            in_specs=[pl.BlockSpec(memory_space=pltpu.SMEM), vmem, vmem, vmem, vmem],
-            out_specs=vmem,
+            out_shape=pltpu.VMEM((slots, 2, cycle), jnp.float32),
+            in_specs=[place] * 5,
+            out_specs=pl.BlockSpec(memory_space=pltpu.VMEM),
             scratch_shapes=[
+                pltpu.SMEM(assignment.shape, jnp.int32),
+                pltpu.VMEM(database.shape, jnp.int32),
+                pltpu.VMEM(queries.shape, jnp.int32),
+                pltpu.VMEM(key_rows.shape, jnp.int32),
+                pltpu.VMEM(hint.shape, jnp.int32),
+                pltpu.SemaphoreType.DMA((5,)),
                 pltpu.VMEM((polys * rows * clients, LANES), jnp.int32),
                 pltpu.VMEM((polys * clients, rows, LANES), jnp.int32),
                 pltpu.VMEM((polys * clients, tiles, LANES), jnp.int32),
@@ -285,8 +310,10 @@
                 pltpu.SemaphoreType.DMA((n,)),
                 pltpu.SemaphoreType.DMA((n,)),
             ],
-            compiler_params=pltpu.CompilerParams(collective_id=0, has_side_effects=True),
-        )(assignment, database, queries, key_rows, hint)
+            compiler_params=pltpu.CompilerParams(
+                collective_id=0, has_side_effects=True
+            ),
+        )(*(pltpu.with_memory_space_constraint(x, pltpu.HBM) for x in (assignment, database, queries, key_rows, hint)))
 
     placed = (P("col", "grp"), P("grp", "col"), P("grp", "col"), P("grp", None), P("grp"))
     return jax.shard_map(

time: 13.5 us -> 11.7 us (0.87)
  Pallas kernels: 12 us -> 10.9 us
  local copies, waits for them, and re-layouts: 1.3 us -> 0.6 us
    pallas_call x1, Pallas kernels: 12 us -> 10.9 us  [on_device(): pl.pallas_call(functools.partial(kernel, n, slots, share), out_shape=pltp...]
    unnamed x1, local copies, waits for them, and re-layouts: 1.3 us -> 0.6 us
where the time goes in v2:
time: 11.7 us; the launch traced here: 11.5 us
  Pallas kernels  10.9 us (93%)
  local copies, waits for them, and re-layouts  0.6 us (5%)
    pallas_call x1, Pallas kernels, on_device(): pl.pallas_call(functools.partial(kernel, n, slots, share), out_shape=pltp...  10.9 us
    unnamed x1, local copies, waits for them, and re-layouts  0.6 us

profile of v2, /device:TPU:0, one launch (start us, length us, event | category | flops | bytes accessed | tf_op | source)
XLA Modules:
  0.0 11.5 jit_solution(16581230128857301995)
XLA Ops:
  0.0 10.9 %shard_map.55 = f32[1,2,1024]{2,1,0:T(2,128)S(1)} custom-call(s32[16]{0:T(128)} %assign_hbm.1, s32[16,2048]{1,0:T(8,128)} %database_hbm.1, s32[8,16]{1,0:T(8,128)} %queries_hbm.1, s32[8,512]{1,0:T(8,128)} %keys_hbm.1, s32[2,1024]{1,0:T(2,128)} %hint_hbm.1), custom_call_target="tpu_custom_call" | custom-call | tf_op jit(solution)/shard_map/pallas_call | solution.py:286
  10.9 0.6 %copy.7 = f32[1,2,1024]{2,1,0:T(2,128)} copy(f32[1,2,1024]{2,1,0:T(2,128)S(1)} %shard_map.55) | data formatting | bytes 16384
